TPU v7x, 512 devices: a whole 4x8x8 slice. The times are simulated.
512 devices in a mesh: pair: 64 (over z, x, core), cuts: 8 (over y).
Axes of the slice: x: 4, y: 8, z: 8, core: 2. Of those that a mesh axis runs over, the one named last changes fastest.
Arguments:
- amplitudes: bfloat16 [65536, 2048], P('pair'), may hold values from -6 to 6
- factors: bfloat16 [128, 24, 128, 128], P('pair', 'cuts'), may hold values from -0.5 to 0.5
- screening: int32 [32, 16], replicated, may hold values from 0 to 127, as said below
- tile_slot: int32 [128], replicated, may hold values from 0 to 127, as said below
- pair_orbitals: int32 [32, 2], replicated, may hold values from 0 to 3999
- occupied_energy: float32 [4000], replicated, may hold values from -2 to -0.3
- virtual_energy: float32 [128, 128], replicated, may hold values from 0.2 to 3
Outputs:
- scaled_residual: float32 [65536, 2048], P(('pair', 'cuts'))
Inputs may be any that keep to these rules, and one draw needn't show every extreme that they name: `screening`: call tile_slot[t] // 2 the owner of tile t. The 16 tiles named by one pair have 16 different owners. `tile_slot`: every tile has its own slot.
All inputs are finite; a program needn't handle non-finite values.
Results may differ from a plain program's by a relative error of at most 0.012.
Values may be sent and summed in bfloat16 or wider, within the bound.
A program may use at most 64 MiB of HBM per device.

v0:
```python
import jax
import jax.numpy as jnp
from jax import lax
from jax.sharding import PartitionSpec as P

TILE = 128
K = 16
NQ_CUT = 3


def local(
    amplitudes, factors, screening, tile_slot, pair_orbitals, occupied_energy, virtual_energy
):
    pair_index = lax.axis_index("pair")
    row_tiles = amplitudes.shape[0] // TILE
    first_tile = pair_index * row_tiles
    pair_id = first_tile // K
    tile_start = first_tile % K
    my_tiles = lax.dynamic_slice_in_dim(screening, pair_id, 1, 0).reshape(K)
    my_slots = tile_slot[my_tiles]
    segment = lax.all_gather(factors, "pair", axis=0, tiled=True)
    count = segment.shape[0]
    inside = (my_slots >= 0) & (my_slots < count)
    safe_rows = jnp.clip(my_slots, 0, count - 1)
    picked = jnp.where(inside[:, None, None, None], segment[safe_rows], jnp.zeros((), jnp.bfloat16))
    left_tiles = lax.dynamic_slice_in_dim(picked, tile_start, row_tiles, 0)
    blocks = amplitudes.reshape(row_tiles, TILE, K * TILE)
    running = jnp.zeros((row_tiles, TILE, K, TILE), jnp.float32)
    for vector in range(NQ_CUT):
        factor_left = left_tiles[:, vector]
        half_done = jnp.einsum(
            "iac,icx->iax", factor_left, blocks, preferred_element_type=jnp.float32
        )
        half_done = half_done.astype(jnp.bfloat16).reshape(row_tiles, TILE, K, TILE)
        running = running + jnp.einsum(
            "iajd,jbd->iajb", half_done, picked[:, vector], preferred_element_type=jnp.float32
        )
    partial_value = running.reshape(row_tiles * TILE, K * TILE)
    summed = lax.psum_scatter(
        partial_value.astype(jnp.bfloat16), "cuts", scatter_dimension=0, tiled=True
    ).astype(jnp.float32)
    orbitals = lax.dynamic_slice_in_dim(pair_orbitals, pair_id, 1, 0).reshape(2)
    pair_energy = occupied_energy[orbitals]
    tile_energy = virtual_energy[my_tiles].reshape(K * TILE)
    row_energy = tile_energy - pair_energy[0]
    col_energy = tile_energy - pair_energy[1]
    row_count = summed.shape[0]
    row_begin = tile_start * TILE + lax.axis_index("cuts") * row_count
    row_part = lax.dynamic_slice_in_dim(row_energy, row_begin, row_count, 0)
    return summed / (row_part[:, None] + col_energy[None, :])


def solution(mesh):
    return jax.shard_map(
        local,
        mesh=mesh,
        in_specs=(P("pair", None), P("pair", "cuts", None, None), P(), P(), P(), P(), P()),
        out_specs=P(("pair", "cuts"), None),
        check_vma=False,
    )
```

profile of v0, /device:TPU:1, one launch (start us, length us, event | category | flops | bytes accessed | tf_op | source)
XLA Modules:
  0.0 212.6 jit_solution(11448872017577413834)
XLA Ops:
  6.5 0.7 all-gather.2.cloned.1.call-update
  7.3 0.0 reduce-scatter.2.cloned.1.call-start
  7.3 0.9 dynamic-slice_reduce_fusion
  8.2 1.3 gather_fusion
  9.6 103.0 %all-gather.2.cloned.1.call-done = bf16[128,3,128,128]{3,2,1,0:T(8,128)(2,1)} async-done(((bf16[2,3,128,128]{3,2,1,0:T(8,128)(2,1)}), bf16[128,3,128,128]{3,2,1,0:T(8,128)(2,1)}) %all-gather.2.cloned.1.call-update) | async-done | bytes 12582928 | tf_op jit(solution)/shard_map/all_gather | solution.py:21
  112.6 5.4 %gather_fusion.1 = bf16[16,3,128,128]{3,2,1,0:T(8,128)(2,1)S(1)} fusion(bf16[128,3,128,128]{3,2,1,0:T(8,128)(2,1)} %all-gather.2.cloned.1.call-done, s32[1024]{0:T(1024)S(1)} %pad_clamp_fusion.1), kind=kCustom, calls=%fused_computation.1 | custom fusion | bytes 3145792 | tf_op jit(solution)/shard_map/gather | solution.py:25
  118.0 0.2 copy_select_fusion
  118.2 4.0 %convert_bitcast_fusion.2 = bf16[8,16,16,8,128]{4,3,2,1,0:T(8,128)(2,1)S(1)} fusion(bf16[8,128,2048]{2,1,0:T(8,128)(2,1)} %bitcast.73, bf16[16,3,128,128]{3,2,0,1:T(8,128)(2,1)S(1)} %copy_select_fusion, s32[]{:T(128)S(6)} %select_n.62), kind=kOutput, calls=%fused_computation.18 | convolution fusion | flops 538968064 | bytes 8650756 | tf_op jit(solution)/shard_map/iac,icx->iax/dot_general | solution.py:31
  122.3 1.2 convert_bitcast_fusion.1
  123.5 1.3 fusion.4
  124.9 1.2 convert_bitcast_fusion
  126.1 4.5 %fusion.1 = f32[16,128,8,128]{3,1,2,0:T(8,128)} fusion(bf16[8,16,16,8,128]{4,3,2,1,0:T(8,128)(2,1)S(1)} %convert_bitcast_fusion, bf16[16,3,128,128]{3,2,0,1:T(8,128)(2,1)S(1)} %copy_select_fusion), kind=kOutput, calls=%fused_computation.7 | convolution fusion | flops 536870912 | bytes 13107200 | tf_op jit(solution)/shard_map/iajd,jbd->iajb/dot_general | solution.py:35
  130.6 5.9 %fusion = bf16[8,128,16,128]{1,3,0,2:T(8,128)(2,1)} fusion(f32[16,128,8,128]{3,1,2,0:T(8,128)} %fusion.1, f32[16,128,8,128]{3,1,2,0:T(8,128)S(1)} %fusion.4, bf16[8,16,16,8,128]{4,3,2,1,0:T(8,128)(2,1)S(1)} %convert_bitcast_fusion.2, bf16[16,3,128,128]{3,2,0,1:T(8,128)(2,1)} %copy-done.3), kind=kOutput, calls=%fused_computation.5 | convolution fusion | flops 543162368 | bytes 25690112 | tf_op jit(solution)/shard_map/iajd,jbd->iajb/dot_general | solution.py:35
  136.5 6.8 %copy.20 = bf16[8,128,16,128]{3,2,1,0:T(8,128)(2,1)} copy(bf16[8,128,16,128]{1,3,0,2:T(8,128)(2,1)} %fusion) | data formatting | bytes 8388608 | tf_op jit(solution)/shard_map/convert_element_type | solution.py:40
  143.3 6.2 %copy.44 = bf16[128,8,16,128]{3,1,2,0:T(8,128)(2,1)} copy(bf16[128,8,16,128]{3,2,1,0:T(8,128)(2,1)} %bitcast.77) | data formatting | bytes 8388608
  149.6 0.6 gather_fusion.2
  150.2 0.1 copy-done.4
  150.3 0.2 fusion.15
  150.5 0.6 gather_fusion.3
  151.1 0.6 fusion.19
  151.7 1.3 subtract_bitcast_fusion.1
  153.0 0.1 dynamic_slice.15
  153.1 50.4 %reduce-scatter.2.cloned.1.call-done = bf16[128,2048]{1,0:T(8,128)(2,1)} async-done(((bf16[1024,2048]{1,0:T(8,128)(2,1)}), bf16[128,2048]{1,0:T(8,128)(2,1)}) %reduce-scatter.2.cloned.1.call-update) | async-done | bytes 524304 | tf_op jit(solution)/shard_map/reduce_scatter | solution.py:39
  203.5 2.2 %add_divide_fusion = f32[128,2048]{1,0:T(8,128)} fusion(bf16[128,2048]{1,0:T(8,128)(2,1)} %reduce-scatter.2.cloned.1.call-done, f32[2048]{0:T(1024)S(1)} %get-tuple-element.6, f32[128]{0:T(128)S(1)} %dynamic_slice.15), kind=kLoop, calls=%fused_computation.20 | loop fusion | flops 786432 | bytes 1581568 | tf_op jit(solution)/shard_map/div | solution.py:50
  (18 shorter events, 0.1 us)
Async XLA Ops:
  6.5 143.1 %copy-start = (f32[128,128]{1,0:T(8,128)S(1)}, f32[128,128]{1,0:T(8,128)}, u32[]{:S(2)}) copy-start(f32[128,128]{1,0:T(8,128)} %param.13) | copy-start | bytes 196612
  6.5 106.1 %all-gather.2.cloned.1.call-start = ((), (), s32[]{:S(2)}) async-start(), calls=%async_computation.1 | async-start | bytes 12779520 | tf_op jit(solution)/shard_map/all_gather | solution.py:21
  7.3 196.3 %reduce-scatter.2.cloned.1.call-start = ((), (), s32[]{:S(2)}) async-start(), calls=%async_computation.2 | async-start | bytes 4718592 | tf_op jit(solution)/shard_map/reduce_scatter | solution.py:39
  118.2 7.9 %copy-start.3 = (bf16[16,3,128,128]{3,2,0,1:T(8,128)(2,1)}, bf16[16,3,128,128]{3,2,0,1:T(8,128)(2,1)S(1)}, u32[]{:S(2)}) copy-start(bf16[16,3,128,128]{3,2,0,1:T(8,128)(2,1)S(1)} %copy_select_fusion) | copy-start | bytes 4718596
  118.2 4.1 %copy-start.1 = (bf16[1024,2048]{1,0:T(8,128)(2,1)S(1)}, bf16[1024,2048]{1,0:T(8,128)(2,1)}, u32[]{:S(2)}) copy-start(bf16[1024,2048]{1,0:T(8,128)(2,1)} %param.7) | copy-start | bytes 12582916
  149.6 0.7 copy-start.4
  149.6 0.9 copy-start.2
Sparse Core Ops, SparseCore 0:
  10.7 101.8 all-gather.1
  149.7 53.7 reduce-scatter.1
where the time goes:
time: 213 us
  waiting for transfers between devices  154 us (72%)
  local copies, waits for them, and re-layouts  22.8 us (11%)
  matrix products  18.3 us (9%)
  between operations  13.6 us (6%)
  other arithmetic  3.71 us (2%)
    all_gather x1, waiting for transfers between devices, local(): segment = lax.all_gather(factors, 'pair', axis=0, tiled=True)  103 us
    reduce_scatter x1, waiting for transfers between devices, local(): lax.psum_scatter(partial_value.astype(jnp.bfloat16), 'cuts', scatter_dime...  50.4 us
    dot_general x3, matrix products, local(): jnp.einsum('iajd,jbd->iajb', half_done, picked[:, vector], preferred_elem...  11.7 us
    convert_element_type x1, local copies, waits for them, and re-layouts, local(): partial_value.astype(jnp.bfloat16)  6.81 us
    dot_general x3, matrix products, local(): jnp.einsum('iac,icx->iax', factor_left, blocks, preferred_element_type=jn...  6.52 us
    unnamed x11, local copies, waits for them, and re-layouts  6.33 us
    gather x1, local copies, waits for them, and re-layouts, local(): segment[safe_rows]  5.42 us
  transfers between devices with their start and end apart: 2, of which 2 were waited for; matrix products, arithmetic and copies ran while one was open for 3% of the time, Pallas kernels for 0%

commit v1 on v0

--- a/solution.py
+++ b/solution.py
@@ -18,7 +18,9 @@
     tile_start = first_tile % K
     my_tiles = lax.dynamic_slice_in_dim(screening, pair_id, 1, 0).reshape(K)
     my_slots = tile_slot[my_tiles]
-    segment = lax.all_gather(factors, "pair", axis=0, tiled=True)
+    segment = jnp.concatenate(
+        lax.all_to_all(jnp.stack([factors] * lax.axis_size("pair")), "pair", 0, 0), axis=0
+    )
     count = segment.shape[0]
     inside = (my_slots >= 0) & (my_slots < count)
     safe_rows = jnp.clip(my_slots, 0, count - 1)

time: 213 us -> 411 us (1.93)
  waiting for transfers between devices: 154 us -> 329 us
  starting transfers between devices: 0.04 us -> 15.4 us
  local copies, waits for them, and re-layouts: 22.8 us -> 30.1 us
    all_to_all x0 -> x1, waiting for transfers between devices: none -> 273 us  [local(): lax.all_to_all(jnp.stack([factors] * lax.axis_size('pair')), 'pair', 0, 0)]
    all_gather x1 -> x0, waiting for transfers between devices: 103 us -> none  [local(): segment = lax.all_gather(factors, 'pair', axis=0, tiled=True)]
    all_to_all x0 -> x1, starting transfers between devices: none -> 15.1 us  [local(): lax.all_to_all(jnp.stack([factors] * lax.axis_size('pair')), 'pair', 0, 0)]
    another operation x0 -> x1, local copies, waits for them, and re-layouts: none -> 8.65 us  [local(): jnp.stack([factors] * lax.axis_size('pair'))]
    reduce_scatter x1, waiting for transfers between devices: 50.4 us -> 55.8 us  [local(): lax.psum_scatter(partial_value.astype(jnp.bfloat16), 'cuts', scatter_dime...]
  transfers between devices with their start and end apart: 2 -> 2, of which waited for: 2 -> 2; matrix products, arithmetic and copies ran while one was open for 3% -> 1% of each run, Pallas kernels for 0% -> 0%
where the time goes in v1:
time: 411 us; the launch traced here: 410 us
  waiting for transfers between devices  329 us (80%)
  local copies, waits for them, and re-layouts  30.1 us (7%)
  matrix products  18.3 us (4%)
  starting transfers between devices  15.4 us (4%)
  between operations  13.6 us (3%)
    all_to_all x1, waiting for transfers between devices, local(): lax.all_to_all(jnp.stack([factors] * lax.axis_size('pair')), 'pair', 0, 0)  273 us
    reduce_scatter x1, waiting for transfers between devices, local(): lax.psum_scatter(partial_value.astype(jnp.bfloat16), 'cuts', scatter_dime...  55.8 us
    all_to_all x1, starting transfers between devices, local(): lax.all_to_all(jnp.stack([factors] * lax.axis_size('pair')), 'pair', 0, 0)  15.1 us
    dot_general x3, matrix products, local(): jnp.einsum('iajd,jbd->iajb', half_done, picked[:, vector], preferred_elem...  11.7 us
    another operation x1, local copies, waits for them, and re-layouts, local(): jnp.stack([factors] * lax.axis_size('pair'))  8.65 us
  transfers between devices with their start and end apart: 2, of which 2 were waited for; matrix products, arithmetic and copies ran while one was open for 1% of the time, Pallas kernels for 0%

profile of v1, /device:TPU:1, one launch (start us, length us, event | category | flops | bytes accessed | tf_op | source)
XLA Modules:
  0.0 410.1 jit_solution(4019707265004323174)
XLA Ops:
  6.5 8.6 %stack.2 = bf16[64,2,3,128,128]{4,3,2,1,0:T(8,128)(2,1)} broadcast(bf16[2,3,128,128]{3,2,1,0:T(8,128)(2,1)} %param.8), dimensions={1,2,3,4} | broadcast | bytes 12779520 | tf_op jit(solution)/shard_map/stack | solution.py:22
  15.2 15.1 %all-to-all-start = ((bf16[64,2,3,128,128]{4,3,2,1,0:T(8,128)(2,1)}), bf16[64,2,3,128,128]{4,3,2,1,0:T(8,128)(2,1)}, u32[]{:S(2)}, u32[]{:S(2)}) async-start(bf16[64,2,3,128,128]{4,3,2,1,0:T(8,128)(2,1)} %stack.2), calls=%async_computation | async-start | bytes 25165824 | tf_op jit(solution)/shard_map/all_to_all | solution.py:22
  30.3 0.2 reduce-scatter.2.cloned.1.call-start
  30.6 0.2 dynamic-slice_reduce_fusion
  30.8 0.7 gather_fusion
  31.5 273.3 %all-to-all-done = bf16[64,2,3,128,128]{4,3,2,1,0:T(8,128)(2,1)} async-done(((bf16[64,2,3,128,128]{4,3,2,1,0:T(8,128)(2,1)}), bf16[64,2,3,128,128]{4,3,2,1,0:T(8,128)(2,1)}, u32[]{:S(2)}, u32[]{:S(2)}) %all-to-all-start) | async-done | bytes 12582944 | tf_op jit(solution)/shard_map/all_to_all | solution.py:22
  304.8 5.4 %gather_fusion.1 = bf16[16,3,128,128]{3,2,1,0:T(8,128)(2,1)S(1)} fusion(bf16[128,3,128,128]{3,2,1,0:T(8,128)(2,1)} %bitcast.1, s32[1024]{0:T(1024)S(1)} %pad_clamp_fusion.1), kind=kCustom, calls=%fused_computation.1 | custom fusion | bytes 3145792 | tf_op jit(solution)/shard_map/gather | solution.py:27
  310.3 0.2 copy_select_fusion
  310.5 4.0 convert_bitcast_fusion.2
  314.5 1.2 convert_bitcast_fusion.1
  315.8 1.3 fusion.4
  317.1 1.2 convert_bitcast_fusion
  318.3 4.5 %fusion.1 = f32[16,128,8,128]{3,1,2,0:T(8,128)} fusion(bf16[8,16,16,8,128]{4,3,2,1,0:T(8,128)(2,1)S(1)} %convert_bitcast_fusion, bf16[16,3,128,128]{3,2,0,1:T(8,128)(2,1)S(1)} %copy_select_fusion), kind=kOutput, calls=%fused_computation.7 | convolution fusion | flops 536870912 | bytes 13107200 | tf_op jit(solution)/shard_map/iajd,jbd->iajb/dot_general | solution.py:37
  322.9 5.9 %fusion = bf16[8,128,16,128]{1,3,0,2:T(8,128)(2,1)} fusion(f32[16,128,8,128]{3,1,2,0:T(8,128)} %fusion.1, f32[16,128,8,128]{3,1,2,0:T(8,128)S(1)} %fusion.4, bf16[8,16,16,8,128]{4,3,2,1,0:T(8,128)(2,1)S(1)} %convert_bitcast_fusion.2, bf16[16,3,128,128]{3,2,0,1:T(8,128)(2,1)} %copy-done.4), kind=kOutput, calls=%fused_computation.5 | convolution fusion | flops 543162368 | bytes 25690112 | tf_op jit(solution)/shard_map/iajd,jbd->iajb/dot_general | solution.py:37
  328.8 6.8 %copy.15 = bf16[8,128,16,128]{3,2,1,0:T(8,128)(2,1)} copy(bf16[8,128,16,128]{1,3,0,2:T(8,128)(2,1)} %fusion) | data formatting | bytes 8388608 | tf_op jit(solution)/shard_map/convert_element_type | solution.py:42
  335.5 6.2 %copy.39 = bf16[128,8,16,128]{3,1,2,0:T(8,128)(2,1)} copy(bf16[128,8,16,128]{3,2,1,0:T(8,128)(2,1)} %bitcast.78) | data formatting | bytes 8388608
  341.8 0.6 gather_fusion.2
  342.5 0.2 fusion.15
  342.7 0.6 gather_fusion.3
  343.3 0.6 fusion.19
  343.9 1.3 subtract_bitcast_fusion.1
  345.2 0.1 dynamic_slice.15
  345.3 55.8 %reduce-scatter.2.cloned.1.call-done = bf16[128,2048]{1,0:T(8,128)(2,1)} async-done(((bf16[1024,2048]{1,0:T(8,128)(2,1)}), bf16[128,2048]{1,0:T(8,128)(2,1)}) %reduce-scatter.2.cloned.1.call-update) | async-done | bytes 524304 | tf_op jit(solution)/shard_map/reduce_scatter | solution.py:41
  401.1 2.2 add_divide_fusion
  (22 shorter events, 0.2 us)
Async XLA Ops:
  6.5 335.3 %copy-start = (f32[128,128]{1,0:T(8,128)S(1)}, f32[128,128]{1,0:T(8,128)}, u32[]{:S(2)}) copy-start(f32[128,128]{1,0:T(8,128)} %param.13) | copy-start | bytes 196612
  15.2 15.4 %copy-start.5 = (s32[32,16]{0,1:T(8,128)S(1)}, s32[32,16]{0,1:T(8,128)}, u32[]{:S(2)}) copy-start(s32[32,16]{0,1:T(8,128)} %param.9) | copy-start | bytes 6148
  15.2 15.6 %copy-start.1 = (s32[128]{0:T(128)S(1)}, s32[128]{0:T(128)}, u32[]{:S(2)}) copy-start(s32[128]{0:T(128)} %param.10) | copy-start | bytes 1540
  15.2 289.6 %all-to-all-start = ((bf16[64,2,3,128,128]{4,3,2,1,0:T(8,128)(2,1)}), bf16[64,2,3,128,128]{4,3,2,1,0:T(8,128)(2,1)}, u32[]{:S(2)}, u32[]{:S(2)}) async-start(bf16[64,2,3,128,128]{4,3,2,1,0:T(8,128)(2,1)} %stack.2), calls=%async_computation | async-start | bytes 25165824 | tf_op jit(solution)/shard_map/all_to_all | solution.py:22
  30.3 370.7 %reduce-scatter.2.cloned.1.call-start = ((), (), s32[]{:S(2)}) async-start(), calls=%async_computation.2 | async-start | bytes 4718592 | tf_op jit(solution)/shard_map/reduce_scatter | solution.py:41
  310.4 7.9 %copy-start.4 = (bf16[16,3,128,128]{3,2,0,1:T(8,128)(2,1)}, bf16[16,3,128,128]{3,2,0,1:T(8,128)(2,1)S(1)}, u32[]{:S(2)}) copy-start(bf16[16,3,128,128]{3,2,0,1:T(8,128)(2,1)S(1)} %copy_select_fusion) | copy-start | bytes 4718596
  310.4 4.1 copy-start.2
  341.8 0.7 copy-start.6
  341.8 0.9 copy-start.3
Sparse Core Ops, SparseCore 0:
  341.9 59.0 reduce-scatter.1
